TPU v7x, 32 devices: a whole 2x2x4 slice. The times are simulated.
32 devices in a mesh: elem: 8 (over y, x, core), mode: 4 (over z).
Axes of the slice: x: 2, y: 2, z: 4, core: 2. Of those that a mesh axis runs over, the one named last changes fastest.
Arguments:
- velocity: float32 [3, 5184, 2, 512], P(None, 'elem', None, 'mode'), may hold values from -3 to 3
- column_width: float32 [8], P('elem'), may hold values from 0.5 to 2
- row_height: float32 [8], replicated, may hold values from 0.5 to 2
- disc_mask: int32 [64], P('elem'), may hold values from 0 to 1, as said below
Outputs:
- velocity_new: float32 [3, 5184, 2, 512], P(None, 'elem', None, 'mode')
Inputs may be any that keep to these rules, and one draw needn't show every extreme that they name: `disc_mask`: in each column of 8 elements the ones form one run of 2 to 4 consecutive rows, counted cyclically in y.
All inputs are finite; a program needn't handle non-finite values.
Results may differ from a plain program's by a relative error of at most 0.0001.
Values sent between devices are 32-bit elements; how exact they have to be, the bound alone decides.
A program may use at most 128 MiB of HBM per device.

v0:
```python
import math
import jax
import jax.numpy as jnp
import numpy as np
from jax import lax
from jax.sharding import PartitionSpec as P

ORDER = 8
ITERS = 2
gll_points = [
    -1.0,
    -0.8997579954114602,
    -0.6771862795107377,
    -0.3631174638261782,
    0.0,
    0.3631174638261782,
    0.6771862795107377,
    0.8997579954114602,
    1.0,
]
gll_weights = [
    0.0277777777777778,
    0.1654953615608055,
    0.2745387125001617,
    0.3464285109730463,
    0.3715192743764172,
    0.3464285109730463,
    0.2745387125001617,
    0.1654953615608055,
    0.0277777777777778,
]
viscosity = 0.5
time_step = 0.02
thrust_coef = 4.0 / 3.0
highest = lax.Precision.HIGHEST


def padded(shard, sides, width):
    for axis, dim in sides:
        peers, length = (lax.axis_size(axis), shard.shape[dim])
        up = [(i, (i + 1) % peers) for i in range(peers)]
        down = [(j, i) for i, j in up]
        last = lax.slice_in_dim(shard, length - width, length, axis=dim)
        initial = lax.slice_in_dim(shard, 0, width, axis=dim)
        before = lax.ppermute(last, axis, up)
        after = lax.ppermute(initial, axis, down)
        shard = jnp.concatenate([before, shard, after], axis=dim)
    return shard


def node_tables():
    points = np.array(gll_points)
    identity = np.eye(9)
    differences = points[:, None] - points[None, :] + identity
    barycentric = 1.0 / np.prod(differences, axis=1)
    off_diagonal = barycentric[None, :] / barycentric[:, None] / differences * (1.0 - identity)
    derivative = off_diagonal - identity * off_diagonal.sum(axis=1)[:, None]
    return (
        jnp.asarray(derivative, dtype=jnp.float32),
        jnp.asarray(np.array(gll_weights), dtype=jnp.float32),
    )


def spectral_tables(mode_count):
    planes = 3 * mode_count
    wave_index = jnp.arange(mode_count, dtype=jnp.int32)
    plane_index = jnp.arange(planes, dtype=jnp.int32)
    phase_index = wave_index[:, None] * plane_index[None, :] % planes
    angles = 2.0 * math.pi / planes * phase_index.astype(jnp.float32)
    cosine_table = jnp.cos(angles)
    sine_table = jnp.sin(angles)
    mode_weight = jnp.where(wave_index == 0, 1.0, 2.0).astype(jnp.float32)[:, None] / math.sqrt(
        mode_count
    )
    wave_number = 8.0 / mode_count * wave_index.astype(jnp.float32)[:, None]
    inverse = jnp.concatenate([mode_weight * cosine_table, -mode_weight * sine_table], axis=0)
    spanwise = jnp.concatenate(
        [-wave_number * mode_weight * sine_table, -wave_number * mode_weight * cosine_table], axis=0
    )
    forward = (
        math.sqrt(mode_count) / planes * jnp.concatenate([cosine_table, -sine_table], axis=0).T
    )
    return (inverse, spanwise, forward)


def assemble(nodal_field):
    extended = padded(nodal_field, (("elem", 2),), 1)
    first_layer = nodal_field[:, :, 0] + extended[:, :, 0]
    last_layer = nodal_field[:, :, 8] + extended[:, :, 10]
    nodal_field = jnp.concatenate(
        [first_layer[:, :, None], nodal_field[:, :, 1:8], last_layer[:, :, None]], axis=2
    )
    upper_layer = nodal_field[:, :, :, 8] + jnp.roll(nodal_field[:, :, :, 0], -1, axis=1)
    return jnp.concatenate(
        [
            jnp.roll(upper_layer, 1, axis=1)[:, :, :, None],
            nodal_field[:, :, :, 1:8],
            upper_layer[:, :, :, None],
        ],
        axis=3,
    )


def apply_operator(nodal_field, derivative, quad_weights, ratio_x, ratio_y, jacobian, factor):
    grad_r = jnp.einsum("ij,pejbl->peibl", derivative, nodal_field, precision=highest)
    grad_s = jnp.einsum("ij,peajl->peail", derivative, nodal_field, precision=highest)
    flux_r = grad_r * quad_weights[None, None, :, :, None] * ratio_x[None, :, None, None, None]
    flux_s = grad_s * quad_weights[None, None, :, :, None] * ratio_y[None, :, None, None, None]
    stiffness = jnp.einsum("ji,pejbl->peibl", derivative, flux_r, precision=highest) + jnp.einsum(
        "ji,peajl->peail", derivative, flux_s, precision=highest
    )
    masses = (
        jacobian[None, :, None, None, None] * quad_weights[None, None, :, :, None] * nodal_field
    )
    return assemble(factor * masses + viscosity * stiffness)


def weighted_sum(left_field, right_field, multiplicity):
    return jnp.sum(left_field * right_field * multiplicity[None, None, :, :, None], axis=(1, 2, 3))


def paired(residual, image_field, multiplicity):
    return lax.psum(
        (
            weighted_sum(residual, residual, multiplicity),
            weighted_sum(residual, image_field, multiplicity),
        ),
        "elem",
    )


def on_device(velocity, column_width, row_height, disc_mask):
    derivative, weights = node_tables()
    quad_weights = weights[:, None] * weights[None, :]
    node_index = jnp.arange(9)
    edge_count = jnp.where((node_index == 0) | (node_index == 8), 2.0, 1.0).astype(jnp.float32)
    multiplicity = 1.0 / (edge_count[:, None] * edge_count[None, :])
    groups = lax.axis_size("mode")
    local_modes = velocity.shape[3]
    mode_count = groups * local_modes
    planes = 3 * mode_count
    elements = velocity.shape[1] // 81
    local_elems = elements // groups
    col_width = column_width[0]
    inverse, spanwise, forward = spectral_tables(mode_count)
    nodal_field = velocity.reshape(3, elements, 9, 9, 2 * local_modes)
    mode_index = lax.axis_index("mode") * local_modes + jnp.arange(local_modes, dtype=jnp.int32)
    wavenumber = 8.0 / mode_count * mode_index.astype(jnp.float32)
    elem_start = lax.axis_index("mode") * local_elems
    local_heights = lax.dynamic_slice_in_dim(row_height, elem_start, local_elems)
    local_disc = lax.dynamic_slice_in_dim(disc_mask, elem_start, local_elems).astype(jnp.float32)
    members = lax.all_to_all(velocity, "mode", split_axis=1, concat_axis=3, tiled=True)
    flat_items = members.reshape(members.shape[0], members.shape[1], 2 * mode_count)
    values = jnp.einsum("pnl,lq->pnq", flat_items, inverse, precision=highest)
    along_z = jnp.einsum("pnl,lq->pnq", flat_items, spanwise, precision=highest)
    values = values.reshape(3, local_elems, 9, 9, planes)
    along_z = along_z.reshape(3, local_elems, 9, 9, planes)
    along_x = 2.0 / col_width * jnp.einsum("ij,pejbq->peibq", derivative, values, precision=highest)
    along_y = (2.0 / local_heights)[None, :, None, None, None] * jnp.einsum(
        "ij,peajq->peaiq", derivative, values, precision=highest
    )
    advection = values[0][None] * along_x + values[1][None] * along_y + values[2][None] * along_z
    plane_index = jnp.arange(planes)
    in_disc = ((plane_index >= 3 * planes // 8) & (plane_index < 5 * planes // 8)).astype(
        jnp.float32
    )
    disc_planes = 5 * planes // 8 - 3 * planes // 8
    local_jacobian = col_width * local_heights / 4.0
    node_weight = (local_disc * local_jacobian)[:, None, None] * quad_weights[None]
    partial_total = jnp.sum(node_weight[:, :, :, None] * values[0] * values[0] * in_disc)
    disc_total = lax.psum(partial_total, "mode")
    disc_area = disc_planes * col_width * jnp.sum(disc_mask.astype(jnp.float32) * row_height)
    pressure = disc_total / disc_area
    thrust = (
        -(0.5 * thrust_coef * ORDER)
        * pressure
        / col_width
        * local_disc[:, None, None, None]
        * in_disc
    )
    tendency = jnp.concatenate([(thrust - advection[0])[None], -advection[1:]], axis=0)
    spectral = jnp.einsum("peabq,ql->peabl", tendency, forward, precision=highest)
    spectral = spectral.reshape(3, local_elems * 81, 2, mode_count)
    returned = lax.all_to_all(spectral, "mode", split_axis=3, concat_axis=1, tiled=True)
    u_star = nodal_field + time_step * returned.reshape(3, elements, 9, 9, 2 * local_modes)
    jacobian = col_width * row_height / 4.0
    ratio_x = row_height / col_width
    ratio_y = col_width / row_height
    single = 1.0 / time_step + viscosity * wavenumber * wavenumber
    factor = jnp.concatenate([single, single])
    right_side = (
        assemble(
            jacobian[None, :, None, None, None] * quad_weights[None, None, :, :, None] * u_star
        )
        / time_step
    )
    residual = right_side
    solution = jnp.zeros_like(right_side)
    image_field = apply_operator(
        residual, derivative, quad_weights, ratio_x, ratio_y, jacobian, factor
    )
    norm_now, product = paired(residual, image_field, multiplicity)
    step_size = norm_now / product
    direction = residual
    along_image = image_field
    for iteration in range(ITERS):
        solution = solution + step_size[:, None, None, None, :] * direction
        residual = residual - step_size[:, None, None, None, :] * along_image
        if iteration + 1 < ITERS:
            image_field = apply_operator(
                residual, derivative, quad_weights, ratio_x, ratio_y, jacobian, factor
            )
            norm_next, product = paired(residual, image_field, multiplicity)
            beta_ratio = norm_next / norm_now
            step_size = norm_next / (product - beta_ratio * norm_next / step_size)
            direction = residual + beta_ratio[:, None, None, None, :] * direction
            along_image = image_field + beta_ratio[:, None, None, None, :] * along_image
            norm_now = norm_next
    return solution.reshape(3, elements * 81, 2, local_modes)


def solution(mesh):
    return jax.shard_map(
        on_device,
        mesh=mesh,
        in_specs=(P(None, "elem", None, "mode"), P("elem"), P(), P("elem")),
        out_specs=P(None, "elem", None, "mode"),
        check_vma=False,
    )
```

profile of v0, /device:TPU:0, one launch (start us, length us, event | category | flops | bytes accessed | tf_op | source)
XLA Modules:
  0.0 403.9 jit_solution(6718678095885858187)
XLA Ops:
  0.0 3.6 copy.119
  3.6 6.3 %all-to-all-start = ((f32[3,648,2,128]{3,2,0,1:T(2,128)}), f32[3,648,2,128]{3,2,0,1:T(2,128)S(1)}, u32[]{:S(2)}, u32[]{:S(2)}) async-start(f32[3,648,2,128]{3,2,0,1:T(2,128)} %copy.119), calls=%async_computation | async-start | bytes 3981312 | tf_op jit(solution)/shard_map/all_to_all | solution.py:152
  13.6 14.0 %fusion.61 = (f32[512,1536]{1,0:T(8,128)}, f32[512,1536]{1,0:T(8,128)}) fusion(), kind=kLoop, calls=%fused_computation.87 | loop fusion | flops 7864320 | bytes 6291456 | tf_op jit(solution)/shard_map/cos | solution.py:70
  27.5 14.2 %fusion.63 = (f32[512,1536]{1,0:T(8,128)}, f32[512,1536]{1,0:T(8,128)}) fusion(f32[512]{0:T(512)S(1)} %negate_multiply_fusion), kind=kLoop, calls=%fused_computation.89 | loop fusion | flops 8650752 | bytes 6293504 | tf_op jit(solution)/shard_map/mul | solution.py:78
  41.7 14.2 %fusion.64 = (f32[512,1536]{1,0:T(8,128)}, f32[512,1536]{1,0:T(8,128)}) fusion(f32[512]{0:T(512)S(1)} %fusion.77, f32[512]{0:T(512)S(1)} %select_multiply_fusion), kind=kLoop, calls=%fused_computation.90 | loop fusion | flops 8650752 | bytes 6295552 | tf_op jit(solution)/shard_map/mul | solution.py:76
  57.7 3.6 reshape.205
  61.3 13.4 %fusion.54 = f32[3,162,1536]{2,1,0:T(8,128)S(1)} fusion(f32[3,162,1024]{2,1,0:T(8,128)} %reshape.205, f32[512,1536]{1,0:T(8,128)S(1)} %copy-done.11, f32[512,1536]{1,0:T(8,128)} %get-tuple-element.64), kind=kOutput, calls=%fused_computation.79 | convolution fusion | flops 9174515712 | bytes 11268096 | tf_op jit(solution)/shard_map/pnl,lq->pnq/dot_general | solution.py:154
  74.7 4.0 copy.122
  79.1 2.4 fusion.74
  82.3 2.5 mul.635
  86.9 2.5 mul.641
  89.5 3.5 copy.127
  92.9 13.4 %fusion.53 = f32[3,162,1536]{2,1,0:T(8,128)S(1)} fusion(f32[3,162,1024]{2,1,0:T(8,128)} %reshape.205, f32[512,1536]{1,0:T(8,128)} %get-tuple-element.56, f32[512,1536]{1,0:T(8,128)S(1)} %copy-done.10), kind=kOutput, calls=%fused_computation.78 | convolution fusion | flops 9174515712 | bytes 11268096 | tf_op jit(solution)/shard_map/pnl,lq->pnq/dot_general | solution.py:155
  106.4 4.2 %copy.128 = f32[3,162,1536]{2,0,1:T(4,128)} copy(f32[3,162,1536]{2,1,0:T(8,128)S(1)} %fusion.53) | data formatting | bytes 5971968 | tf_op jit(solution)/shard_map/pnl,lq->pnq/dot_general | solution.py:155
  110.6 12.8 %psum.35 = f32[]{:T(128)} all-reduce(f32[]{:T(128)} %get-tuple-element.35), channel_id=1, replica_groups=mesh['elem'=8,'mode'=4] {'mode'}, use_global_device_ids=true, to_apply=%region_1.2 | all-reduce | flops 1 | bytes 8 | tf_op jit(solution)/shard_map/psum | solution.py:171
  125.6 11.5 %fusion.16 = f32[3,2,9,1536,9]{3,4,2,1,0:T(8,128)} fusion(f32[9,9,1,1,1]{1,0,4,3,2:T(8,128)S(1)} %copy-done.13, f32[3,2,9,9,1536]{4,0,3,2,1:T(4,128)} %bitcast.137), kind=kOutput, calls=%fused_computation.24 | convolution fusion | flops 80621568 | bytes 5972292 | tf_op jit(solution)/shard_map/ij,peajq->peaiq/dot_general | solution.py:159
  137.1 14.2 %fusion.15 = f32[3,2,9,9,1536]{4,2,3,1,0:T(8,128)S(1)} fusion(f32[3,2,9,9,1536]{4,0,3,2,1:T(4,128)S(1)} %bitcast.139, f32[3,2,9,1536,9]{3,4,2,1,0:T(8,128)} %fusion.16, f32[9,9,1,1,1]{1,0,4,3,2:T(8,128)S(1)} %copy-done.13, f32[3,2,9,9,1536]{4,0,3,2,1:T(4,128)S(1)} %bitcast.138, f32[2,9,9,1536]{3,1,2,0:T(8,128)S(1)} %copy-done.3, f32[2]{0:T(128)S(1)} %copy-done.30, ...), kind=kOutput, calls=%fused_computation.20 | convolution fusion | flops 85847040 | bytes 14930256 | tf_op jit(solution)/shard_map/ij,pejbq->peibq/dot_general | solution.py:158
  154.3 17.1 %fusion.7 = f32[3,2,9,9,1024]{4,2,3,1,0:T(8,128)S(1)} fusion(f32[512,1536]{1,0:T(8,128)S(1)} %copy-done.9, f32[512,1536]{1,0:T(8,128)S(1)} %copy-done.8, f32[2,2,9,9,1536]{4,2,3,1,0:T(8,128)S(1)} %slice_negate_fusion, f32[1,2,9,9,1536]{4,2,3,1,0:T(8,128)S(1)} %slice_subtract_fusion), kind=kOutput, calls=%fused_computation.10 | convolution fusion | flops 9176835072 | bytes 11268096 | tf_op jit(solution)/shard_map/peabq,ql->peabl/dot_general | solution.py:182
  172.8 3.1 reshape.208
  176.0 6.6 %copy.132 = f32[3,162,2,512]{1,2,0,3:T(2,128)} copy(f32[3,162,2,512]{3,2,0,1:T(2,128)} %reshape.208) | data formatting | bytes 3981312 | tf_op jit(solution)/shard_map/reshape | solution.py:183
  182.5 4.7 %all-to-all-start.1 = ((f32[3,162,2,512]{1,2,0,3:T(2,128)}), f32[3,162,2,512]{1,2,0,3:T(2,128)}, u32[]{:S(2)}, u32[]{:S(2)}) async-start(f32[3,162,2,512]{1,2,0,3:T(2,128)} %copy.132), calls=%async_computation.1 | async-start | bytes 6291456 | tf_op jit(solution)/shard_map/all_to_all | solution.py:184
  187.2 3.2 reshape.217
  192.3 63.4 %all-to-all-done.1 = f32[3,162,2,512]{1,2,0,3:T(2,128)} async-done(((f32[3,162,2,512]{1,2,0,3:T(2,128)}), f32[3,162,2,512]{1,2,0,3:T(2,128)}, u32[]{:S(2)}, u32[]{:S(2)}) %all-to-all-start.1) | async-done | bytes 1990688 | tf_op jit(solution)/shard_map/all_to_all | solution.py:184
  255.6 5.2 %broadcast_multiply_fusion = f32[3,162,2,512]{1,2,0,3:T(2,128)} fusion(f32[3,162,2,512]{1,2,0,3:T(2,128)} %all-to-all-done.1), kind=kLoop, calls=%fused_computation.101 | loop fusion | flops 497664 | bytes 3981312 | tf_op jit(solution)/shard_map/mul | solution.py:185
  260.8 6.4 %copy.133 = f32[3,162,2,4,128]{4,2,0,1,3:T(2,128)} copy(f32[3,162,2,4,128]{1,2,0,4,3:T(2,128)} %bitcast.140) | data formatting | bytes 3981312 | tf_op jit(solution)/shard_map/mul | solution.py:185
  267.2 4.7 %mul.655 = f32[3,8,9,9,256]{4,0,3,2,1:T(4,128)} reshape(f32[3,4,162,2,128]{4,3,0,2,1:T(2,128)} %bitcast.143) | data formatting | bytes 3981312 | tf_op jit(solution)/shard_map/mul | solution.py:185
  271.9 3.3 fusion.36
  275.6 2.6 collective-permute-start.1
  278.5 3.9 collective-permute-done
  285.0 4.9 %fusion.44 = f32[3,8,9,256,9]{3,4,2,1,0:T(8,128)S(1)} fusion(f32[9,9,1,1,1]{1,0,4,3,2:T(8,128)S(1)} %copy-done.13, f32[3,8,9,9,256]{4,2,3,1,0:T(8,128)S(1)} %copy_multiply_fusion.4), kind=kOutput, calls=%fused_computation.64 | convolution fusion | flops 53747712 | bytes 3981636 | tf_op jit(solution)/shard_map/ij,peajl->peail/dot_general | solution.py:106
  290.0 4.2 %fusion.33 = f32[3,8,9,256,9]{3,4,2,1,0:T(8,128)S(1)} fusion(f32[9,9,1,1,1]{1,0,4,3,2:T(8,128)S(1)} %copy-done.13, f32[3,8,9,256,9]{3,4,2,1,0:T(8,128)S(1)} %fusion.44, f32[8]{0:T(128)S(1)} %copy-done.31, f32[9,9]{1,0:T(8,128)S(1)} %copy-done.17), kind=kOutput, calls=%fused_computation.49 | convolution fusion | flops 54743040 | bytes 3981992 | tf_op jit(solution)/shard_map/ji,peajl->peail/dot_general | solution.py:109
  294.2 3.9 fusion.35
  298.2 5.9 %fusion.32 = f32[3,8,9,9,256]{4,2,0,1,3:T(8,128)S(1)} fusion(f32[3,8,9,256,9]{3,4,2,1,0:T(8,128)S(1)} %fusion.33, f32[8,9,9]{1,0,2:T(8,128)S(1)} %copy-done.22, f32[256]{0:T(256)S(1)} %pad_maximum_fusion.6, f32[3,8,9,1,256]{4,2,0,1,3:T(8,128)S(1)} %maximum_add_fusion.1, f32[3,8,1,9,256]{4,2,0,1,3:T(1,128)S(1)} %get-tuple-element.32, ...), kind=kOutput, calls=%fused_computation.48 | convolution fusion | flops 61212672 | bytes 8408932 | tf_op jit(solution)/shard_map/ji,pejbl->peibl/dot_general | solution.py:109
  307.5 4.4 %collective-permute-done.2 = f32[3,8,1,9,256]{4,2,0,1,3:T(1,128)S(1)} collective-permute-done((f32[3,8,1,9,256]{4,2,0,1,3:T(1,128)S(1)}, f32[3,8,1,9,256]{4,2,0,1,3:T(1,128)S(1)}, u32[]{:S(2)}, u32[]{:S(2)}) %collective-permute-start.2) | collective-permute-done | bytes 221216 | tf_op jit(solution)/shard_map/ppermute | solution.py:45
  316.5 14.7 %all-reduce.1 = (f32[3,256]{1,0:T(4,128)}, f32[3,256]{1,0:T(4,128)}) all-reduce(f32[3,256]{1,0:T(4,128)} %get-tuple-element.8, f32[3,256]{1,0:T(4,128)} %get-tuple-element.7), channel_id=1, replica_groups=mesh['elem'=8,'mode'=4] {'elem'}, use_global_device_ids=true, to_apply=%region_4.5 | all-reduce | flops 1536 | bytes 12288 | tf_op jit(solution)/shard_map/psum | solution.py:123
  332.5 5.0 %multiply_subtract_fusion = (f32[3,8,9,9,256]{4,2,3,1,0:T(8,128)S(1)}, f32[3,8,9,9,256]{4,2,3,1,0:T(8,128)}) fusion(f32[3,256]{1,0:T(4,128)S(1)} %get-tuple-element.14, f32[3,8,9,9,256]{4,2,0,1,3:T(8,128)S(1)} %fusion.25, f32[3,8,9,1,256]{4,2,3,1,0:T(8,128)} %copy-done.7, f32[3,7,9,256]{3,2,0,1:T(8,128)} %copy-done.12, f32[3,1,9,256]{3,2,0,1:T(8,128)} %copy-done.14, ...), kind=kLoop, calls=%fused_computation.72 | loop fusion | flops 2543616 | bytes 7965696 | tf_op jit(solution)/shard_map/sub | solution.py:208
  337.5 4.9 %fusion.39 = f32[3,8,9,256,9]{3,4,2,1,0:T(8,128)S(1)} fusion(f32[9,9,1,1,1]{1,0,4,3,2:T(8,128)S(1)} %copy-done.13, f32[3,8,9,9,256]{4,2,3,1,0:T(8,128)S(1)} %get-tuple-element.25), kind=kOutput, calls=%fused_computation.58 | convolution fusion | flops 53747712 | bytes 3981636 | tf_op jit(solution)/shard_map/ij,peajl->peail/dot_general | solution.py:106
  342.4 3.4 fusion.30
  345.9 4.1 %fusion.28 = f32[3,8,9,256,9]{3,4,2,1,0:T(8,128)S(1)} fusion(f32[9,9,1,1,1]{1,0,4,3,2:T(8,128)S(1)} %copy-done.13, f32[3,8,9,256,9]{3,4,2,1,0:T(8,128)S(1)} %fusion.39, f32[8]{0:T(128)S(1)} %copy-done.32, f32[9,9]{1,0:T(8,128)S(1)} %copy-done.18), kind=kOutput, calls=%fused_computation.42 | convolution fusion | flops 54743040 | bytes 3981992 | tf_op jit(solution)/shard_map/ji,peajl->peail/dot_general | solution.py:109
  350.0 5.2 %fusion.27 = f32[3,8,9,9,256]{4,2,0,1,3:T(8,128)S(1)} fusion(f32[3,8,9,256,9]{3,4,2,1,0:T(8,128)S(1)} %fusion.28, f32[3,8,9,9,256]{4,2,3,1,0:T(8,128)S(1)} %get-tuple-element.25, f32[9,9,1,1,1]{1,0,2,3,4:T(8,128)S(1)} %copy-done.29, f32[3,8,9,9,256]{4,2,3,1,0:T(8,128)S(1)} %fusion.30, f32[256]{0:T(256)S(1)} %copy-done.40, f32[8,9,9]{1,0,2:T(8,128)S(1)} %copy-done.15), kind=kOutput, calls=%fused_computation.41 | convolution fusion | flops 56236032 | bytes 7966564 | tf_op jit(solution)/shard_map/ji,pejbl->peibl/dot_general | solution.py:109
  358.2 2.6 collective-permute-start.5
  360.8 3.0 copy.136
  363.8 4.8 %concatenate.89 = f32[3,648,2,128]{3,2,0,1:T(2,128)} reshape(f32[3,8,9,9,256]{4,0,3,2,1:T(4,128)} %copy.136) | data formatting | bytes 3981312 | tf_op jit(solution)/shard_map/concatenate | solution.py:94
  370.3 5.0 %copy.155 = f32[3,8,9,9,256]{4,0,3,2,1:T(4,128)} copy(f32[3,8,9,9,256]{4,2,3,1,0:T(8,128)} %get-tuple-element.26) | data formatting | bytes 3981312 | tf_op jit(solution)/shard_map/concatenate | solution.py:94
  375.2 4.5 %concatenate.105 = f32[3,648,2,128]{3,2,0,1:T(2,128)} reshape(f32[3,8,9,9,256]{4,0,3,2,1:T(4,128)} %copy.155) | data formatting | bytes 3981312 | tf_op jit(solution)/shard_map/concatenate | solution.py:94
  379.8 2.5 slice_add_fusion.1
  385.7 12.0 %all-reduce = (f32[3,256]{1,0:T(4,128)S(1)}, f32[3,256]{1,0:T(4,128)S(1)}) all-reduce(f32[3,256]{1,0:T(4,128)S(1)} %get-tuple-element.6, f32[3,256]{1,0:T(4,128)S(1)} %get-tuple-element.5), channel_id=1, replica_groups=mesh['elem'=8,'mode'=4] {'elem'}, use_global_device_ids=true, to_apply=%region_8.9 | all-reduce | flops 1536 | bytes 12288 | tf_op jit(solution)/shard_map/psum | solution.py:123
  397.8 3.6 multiply_add_fusion
  (158 shorter events, 37.4 us)
Async XLA Ops:
  0.0 10.6 %copy-start.37 = (f32[9]{0:T(128)S(1)}, f32[9]{0:T(128)}, u32[]{:S(2)}) copy-start(f32[9]{0:T(128)} %constant.72.clone) | copy-start | bytes 112
  0.0 10.7 %copy-start.38 = (f32[8]{0:T(128)S(1)}, f32[8]{0:T(128)}, u32[]{:S(2)}) copy-start(f32[8]{0:T(128)} %param.8) | copy-start | bytes 100
  0.0 10.7 %copy-start.35 = (s32[8]{0:T(128)S(1)}, s32[8]{0:T(128)}, u32[]{:S(2)}) copy-start(s32[8]{0:T(128)} %param.9) | copy-start | bytes 100
  3.6 52.3 %all-to-all-start = ((f32[3,648,2,128]{3,2,0,1:T(2,128)}), f32[3,648,2,128]{3,2,0,1:T(2,128)S(1)}, u32[]{:S(2)}, u32[]{:S(2)}) async-start(f32[3,648,2,128]{3,2,0,1:T(2,128)} %copy.119), calls=%async_computation | async-start | bytes 3981312 | tf_op jit(solution)/shard_map/all_to_all | solution.py:152
  10.7 31.0 %copy-start.16 = (f32[9,9]{1,0:T(8,128)}, f32[9,9]{1,0:T(8,128)S(1)}, u32[]{:S(2)}) copy-start(f32[9,9]{1,0:T(8,128)S(1)} %copy.118) | copy-start | bytes 976
  13.6 65.5 %copy-start.21 = (f32[1536]{0:T(1024)}, f32[1536]{0:T(1024)S(1)}, u32[]{:S(2)}) copy-start(f32[1536]{0:T(1024)S(1)} %fusion.76) | copy-start | bytes 18436
  57.7 3.6 copy-start.11
  89.5 3.5 copy-start.10
  106.3 19.2 %copy-start.13 = (f32[9,9,1,1,1]{1,0,4,3,2:T(8,128)S(1)}, f32[9,9,1,1,1]{1,0,4,3,2:T(8,128)}, u32[]{:S(2)}) copy-start(f32[9,9,1,1,1]{1,0,4,3,2:T(8,128)} %constant.74) | copy-start | bytes 976
  125.6 11.5 %copy-start.2 = (f32[3,162,1536]{2,0,1:T(4,128)S(1)}, f32[3,162,1536]{2,0,1:T(4,128)}, u32[]{:S(2)}) copy-start(f32[3,162,1536]{2,0,1:T(4,128)} %copy.122) | copy-start | bytes 8957956
  125.6 11.5 %copy-start.3 = (f32[2,9,9,1536]{3,1,2,0:T(8,128)S(1)}, f32[2,9,9,1536]{3,1,2,0:T(8,128)}, u32[]{:S(2)}) copy-start(f32[2,9,9,1536]{3,1,2,0:T(8,128)} %copy.127) | copy-start | bytes 2985988
  125.6 11.5 %copy-start.5 = (f32[3,162,1536]{2,0,1:T(4,128)S(1)}, f32[3,162,1536]{2,0,1:T(4,128)}, u32[]{:S(2)}) copy-start(f32[3,162,1536]{2,0,1:T(4,128)} %copy.128) | copy-start | bytes 8957956
  125.6 11.5 %copy-start.30 = (f32[2]{0:T(128)S(1)}, f32[2]{0:T(128)}, u32[]{:S(2)}) copy-start(f32[2]{0:T(128)} %get-tuple-element.62) | copy-start | bytes 28
  151.4 1.9 copy-start.9
  151.8 2.5 copy-start.8
  182.5 73.1 %all-to-all-start.1 = ((f32[3,162,2,512]{1,2,0,3:T(2,128)}), f32[3,162,2,512]{1,2,0,3:T(2,128)}, u32[]{:S(2)}, u32[]{:S(2)}) async-start(f32[3,162,2,512]{1,2,0,3:T(2,128)} %copy.132), calls=%async_computation.1 | async-start | bytes 6291456 | tf_op jit(solution)/shard_map/all_to_all | solution.py:184
  275.5 6.8 %collective-permute-start = (f32[3,8,1,9,256]{4,2,0,1,3:T(1,128)S(1)}, f32[3,8,1,9,256]{4,2,0,1,3:T(1,128)S(1)}, u32[]{:S(2)}, u32[]{:S(2)}) collective-permute-start(f32[3,8,1,9,256]{4,2,0,1,3:T(1,128)S(1)} %get-tuple-element.33), channel_id=1, source_target_pairs={{0,4},{4,8},{8,12},{12,16},{16,20},{20,24},{24,28},{28,0},{1,5},{5... | collective-permute-start | bytes 663560 | tf_op jit(solution)/shard_map/ppermute | solution.py:45
  275.6 6.8 %collective-permute-start.1 = (f32[3,8,1,9,256]{4,2,0,1,3:T(1,128)S(1)}, f32[3,8,1,9,256]{4,2,0,1,3:T(1,128)S(1)}, u32[]{:S(2)}, u32[]{:S(2)}) collective-permute-start(f32[3,8,1,9,256]{4,2,0,1,3:T(1,128)S(1)} %get-tuple-element.34), channel_id=1, source_target_pairs={{4,0},{8,4},{12,8},{16,12},{20,16},{24,20},{28,24},{0,28},{5,1},{9... | collective-permute-start | bytes 663560 | tf_op jit(solution)/shard_map/ppermute | solution.py:46
  278.2 19.9 %copy-start.39 = (f32[256]{0:T(256)}, f32[256]{0:T(256)S(1)}, u32[]{:S(2)}) copy-start(f32[256]{0:T(256)S(1)} %pad_maximum_fusion.6) | copy-start | bytes 3076
  285.0 4.9 %copy-start.17 = (f32[9,9]{1,0:T(8,128)S(1)}, f32[9,9]{1,0:T(8,128)}, u32[]{:S(2)}) copy-start(f32[9,9]{1,0:T(8,128)} %copy-done.16) | copy-start | bytes 976
  285.0 4.9 %copy-start.31 = (f32[8]{0:T(128)S(1)}, f32[8]{0:T(128)}, u32[]{:S(2)}) copy-start(f32[8]{0:T(128)} %get-tuple-element.57) | copy-start | bytes 100
  290.0 4.2 %copy-start.33 = (f32[8]{0:T(128)S(1)}, f32[8]{0:T(128)}, u32[]{:S(2)}) copy-start(f32[8]{0:T(128)} %get-tuple-element.60) | copy-start | bytes 100
  294.1 4.0 copy-start.22
  294.2 4.0 copy-start.28
  298.1 9.1 %copy-start.36 = (f32[9]{0:T(128)S(1)}, f32[9]{0:T(128)}, u32[]{:S(2)}) copy-start(f32[9]{0:T(128)} %or_select_fusion) | copy-start | bytes 112
  304.3 7.6 %collective-permute-start.2 = (f32[3,8,1,9,256]{4,2,0,1,3:T(1,128)S(1)}, f32[3,8,1,9,256]{4,2,0,1,3:T(1,128)S(1)}, u32[]{:S(2)}, u32[]{:S(2)}) collective-permute-start(f32[3,8,1,9,256]{4,2,0,1,3:T(1,128)S(1)} %get-tuple-element.29), channel_id=1, source_target_pairs={{0,4},{4,8},{8,12},{12,16},{16,20},{20,24},{24,28},{28,0},{1,5},{5... | collective-permute-start | bytes 663560 | tf_op jit(solution)/shard_map/ppermute | solution.py:45
  306.1 5.8 %collective-permute-start.3 = (f32[3,8,1,9,256]{4,2,0,1,3:T(1,128)S(1)}, f32[3,8,1,9,256]{4,2,0,1,3:T(1,128)S(1)}, u32[]{:S(2)}, u32[]{:S(2)}) collective-permute-start(f32[3,8,1,9,256]{4,2,0,1,3:T(1,128)S(1)} %get-tuple-element.30), channel_id=1, source_target_pairs={{4,0},{8,4},{12,8},{16,12},{20,16},{24,20},{28,24},{0,28},{5,1},{9... | collective-permute-start | bytes 663560 | tf_op jit(solution)/shard_map/ppermute | solution.py:46
  307.3 6.2 %copy-start.19 = (f32[9,9]{0,1:T(8,128)}, f32[9,9]{0,1:T(8,128)S(1)}, u32[]{:S(2)}) copy-start(f32[9,9]{0,1:T(8,128)S(1)} %multiply_divide_fusion) | copy-start | bytes 976
  313.4 3.1 copy-start.12
  313.4 3.0 copy-start.14
  314.6 1.9 copy-start.7
  332.5 5.0 %copy-start.23 = (f32[3,256]{1,0:T(4,128)}, f32[3,256]{1,0:T(4,128)S(1)}, u32[]{:S(2)}) copy-start(f32[3,256]{1,0:T(4,128)S(1)} %get-tuple-element.14) | copy-start | bytes 9220
  337.5 12.5 %copy-start = (f32[3,8,9,9,256]{4,2,3,1,0:T(8,128)}, f32[3,8,9,9,256]{4,2,3,1,0:T(8,128)S(1)}, u32[]{:S(2)}) copy-start(f32[3,8,9,9,256]{4,2,3,1,0:T(8,128)S(1)} %get-tuple-element.25) | copy-start | bytes 5971972
  337.5 4.9 %copy-start.34 = (f32[8]{0:T(128)S(1)}, f32[8]{0:T(128)}, u32[]{:S(2)}) copy-start(f32[8]{0:T(128)} %get-tuple-element.60) | copy-start | bytes 100
  342.4 3.4 copy-start.18
  342.4 3.4 copy-start.32
  345.8 4.2 %copy-start.15 = (f32[8,9,9]{1,0,2:T(8,128)S(1)}, f32[8,9,9]{1,0,2:T(8,128)}, u32[]{:S(2)}) copy-start(f32[8,9,9]{1,0,2:T(8,128)} %get-tuple-element.52) | copy-start | bytes 7780
  345.8 4.2 %copy-start.29 = (f32[9,9,1,1,1]{1,0,2,3,4:T(8,128)S(1)}, f32[9,9,1,1,1]{1,0,2,3,4:T(8,128)}, u32[]{:S(2)}) copy-start(f32[9,9,1,1,1]{1,0,2,3,4:T(8,128)} %constant.75) | copy-start | bytes 976
  345.9 4.2 %copy-start.40 = (f32[256]{0:T(256)S(1)}, f32[256]{0:T(256)}, u32[]{:S(2)}) copy-start(f32[256]{0:T(256)} %copy-done.39) | copy-start | bytes 3076
  355.3 1.9 copy-start.6
  358.2 21.6 %collective-permute-start.4 = (f32[3,8,1,9,256]{4,2,0,1,3:T(1,128)}, f32[3,8,1,9,256]{4,2,0,1,3:T(1,128)}, u32[]{:S(2)}, u32[]{:S(2)}) collective-permute-start(f32[3,8,1,9,256]{4,2,0,1,3:T(1,128)} %get-tuple-element.23), channel_id=1, source_target_pairs={{0,4},{4,8},{8,12},{12,16},{16,20},{20,24},{24,28},{28,0},{1,5},{5... | collective-permute-start | bytes 663560 | tf_op jit(solution)/shard_map/ppermute | solution.py:45
  358.2 21.6 %collective-permute-start.5 = (f32[3,8,1,9,256]{4,2,0,1,3:T(1,128)}, f32[3,8,1,9,256]{4,2,0,1,3:T(1,128)}, u32[]{:S(2)}, u32[]{:S(2)}) collective-permute-start(f32[3,8,1,9,256]{4,2,0,1,3:T(1,128)} %get-tuple-element.24), channel_id=1, source_target_pairs={{4,0},{8,4},{12,8},{16,12},{20,16},{24,20},{28,24},{0,28},{5,1},{9... | collective-permute-start | bytes 663560 | tf_op jit(solution)/shard_map/ppermute | solution.py:46
  363.8 6.5 %copy-start.24 = (f32[3,256]{1,0:T(4,128)S(1)}, f32[3,256]{1,0:T(4,128)}, u32[]{:S(2)}) copy-start(f32[3,256]{1,0:T(4,128)} %copy-done.23) | copy-start | bytes 9220
  375.2 4.5 %copy-start.25 = (f32[3,256]{1,0:T(4,128)S(1)}, f32[3,256]{1,0:T(4,128)}, u32[]{:S(2)}) copy-start(f32[3,256]{1,0:T(4,128)} %get-tuple-element.13) | copy-start | bytes 9220
  382.3 2.0 copy-start.1
  382.3 2.0 copy-start.20
  384.3 13.4 %copy-start.26 = (f32[3,256]{1,0:T(4,128)S(1)}, f32[3,256]{1,0:T(4,128)}, u32[]{:S(2)}) copy-start(f32[3,256]{1,0:T(4,128)} %get-tuple-element.11) | copy-start | bytes 9220
  384.3 13.4 %copy-start.27 = (f32[3,256]{1,0:T(4,128)S(1)}, f32[3,256]{1,0:T(4,128)}, u32[]{:S(2)}) copy-start(f32[3,256]{1,0:T(4,128)} %get-tuple-element.12) | copy-start | bytes 9220
  (1 other events, 1.5 us)
where the time goes:
time: 409 us; the launch traced here: 404 us
  matrix products  106 us (26%)
  local copies, waits for them, and re-layouts  84.7 us (21%)
  other arithmetic  79.2 us (19%)
  waiting for transfers between devices  71.7 us (18%)
  blocking collectives  39.5 us (10%)
  starting transfers between devices  19.2 us (5%)
    all_to_all x1, waiting for transfers between devices, on_device(): lax.all_to_all(spectral, 'mode', split_axis=3, concat_axis=1, tiled=True)  63.4 us
    psum x2, blocking collectives, paired(): lax.psum((weighted_sum(residual, residual, multiplicity), weighted_sum(re...  26.7 us
    concatenate x4, local copies, waits for them, and re-layouts, assemble(): jnp.concatenate([jnp.roll(upper_layer, 1, axis=1)[:, :, :, None], nodal_f...  17.2 us
    dot_general x1, matrix products, on_device(): jnp.einsum('peabq,ql->peabl', tendency, forward, precision=highest)  17.1 us
    dot_general x1, matrix products, on_device(): jnp.einsum('ij,pejbq->peibq', derivative, values, precision=highest)  14.2 us
    mul x2, other arithmetic, spectral_tables(): -wave_number * mode_weight * sine_table  14.2 us
    mul x1, other arithmetic, spectral_tables(): -mode_weight * sine_table  14.2 us
    cos x1, other arithmetic, spectral_tables(): cosine_table = jnp.cos(angles)  14 us
  transfers between devices with their start and end apart: 8, of which 3 were waited for; matrix products, arithmetic and copies ran while one was open for 17% of the time, Pallas kernels for 0%

commit v1 on v0

--- a/solution.py
+++ b/solution.py
@@ -33,6 +33,22 @@
 time_step = 0.02
 thrust_coef = 4.0 / 3.0
 highest = lax.Precision.HIGHEST
+
+
+def pairwise_exchange(x, axis, split, join):
+    ways, here = (lax.axis_size(axis), lax.axis_index(axis))
+    width = x.shape[split] // ways
+    shape = list(x.shape)
+    shape[split] = width
+    height = shape[join]
+    shape[join] = height * ways
+    full = jnp.zeros(shape, x.dtype)
+    for mask in range(ways):
+        part = lax.dynamic_slice_in_dim(x, (here ^ mask) * width, width, axis=split)
+        if mask:
+            part = lax.ppermute(part, axis, [(d, d ^ mask) for d in range(ways)])
+        full = lax.dynamic_update_slice_in_dim(full, part, (here ^ mask) * height, axis=join)
+    return full
 
 
 def padded(shard, sides, width):
@@ -181,7 +197,7 @@
     tendency = jnp.concatenate([(thrust - advection[0])[None], -advection[1:]], axis=0)
     spectral = jnp.einsum("peabq,ql->peabl", tendency, forward, precision=highest)
     spectral = spectral.reshape(3, local_elems * 81, 2, mode_count)
-    returned = lax.all_to_all(spectral, "mode", split_axis=3, concat_axis=1, tiled=True)
+    returned = pairwise_exchange(spectral, "mode", 3, 1)
     u_star = nodal_field + time_step * returned.reshape(3, elements, 9, 9, 2 * local_modes)
     jacobian = col_width * row_height / 4.0
     ratio_x = row_height / col_width

time: 409 us -> 376 us (0.919)
  the two profiles are of different devices: /device:TPU:0 before, /device:TPU:12 now
where the time goes in v1:
time: 376 us; the launch traced here: 369 us
  matrix products  106 us (28%)
  other arithmetic  85.7 us (23%)
  local copies, waits for them, and re-layouts  72.4 us (19%)
  waiting for transfers between devices  48.9 us (13%)
  blocking collectives  34.5 us (9%)
  starting transfers between devices  18.1 us (5%)
    ppermute x3, waiting for transfers between devices, pairwise_exchange(): part = lax.ppermute(part, axis, [(d, d ^ mask) for d in range(ways)])  38.3 us
    psum x2, blocking collectives, paired(): lax.psum((weighted_sum(residual, residual, multiplicity), weighted_sum(re...  25 us
    dot_general x1, matrix products, on_device(): jnp.einsum('peabq,ql->peabl', tendency, forward, precision=highest)  17.4 us
    concatenate x4, local copies, waits for them, and re-layouts, assemble(): jnp.concatenate([jnp.roll(upper_layer, 1, axis=1)[:, :, :, None], nodal_f...  17.2 us
    mul x2, other arithmetic, spectral_tables(): -wave_number * mode_weight * sine_table  14.1 us
    dot_general x1, matrix products, on_device(): jnp.einsum('ij,pejbq->peibq', derivative, values, precision=highest)  14 us
    cos x1, other arithmetic, spectral_tables(): cosine_table = jnp.cos(angles)  13.9 us
    dot_general x1, matrix products, on_device(): along_z = jnp.einsum('pnl,lq->pnq', flat_items, spanwise, precision=highest)  13.4 us
  transfers between devices with their start and end apart: 10, of which 5 were waited for; matrix products, arithmetic and copies ran while one was open for 21% of the time, Pallas kernels for 0%

profile of v1, /device:TPU:12, one launch (start us, length us, event | category | flops | bytes accessed | tf_op | source)
XLA Modules:
  0.0 369.0 jit_solution(12019043204662519583)
XLA Ops:
  0.0 3.6 copy.80
  3.6 5.3 %all-to-all-start = ((f32[3,648,2,128]{3,2,0,1:T(2,128)}), f32[3,648,2,128]{3,2,0,1:T(2,128)S(1)}, u32[]{:S(2)}, u32[]{:S(2)}) async-start(f32[3,648,2,128]{3,2,0,1:T(2,128)} %copy.80), calls=%async_computation | async-start | bytes 3981312 | tf_op jit(solution)/shard_map/all_to_all | solution.py:168
  12.3 13.9 %fusion.60 = (f32[512,1536]{1,0:T(8,128)}, f32[512,1536]{1,0:T(8,128)}) fusion(), kind=kLoop, calls=%fused_computation.86 | loop fusion | flops 7864320 | bytes 6291456 | tf_op jit(solution)/shard_map/cos | solution.py:86
  26.3 12.8 %fusion.63 = f32[512,1536]{1,0:T(8,128)} fusion(f32[512]{0:T(512)S(1)} %get-tuple-element.68), kind=kLoop, calls=%fused_computation.89 | loop fusion | flops 7864320 | bytes 3147776 | tf_op jit(solution)/shard_map/mul | solution.py:92
  39.1 12.7 %fusion.71 = f32[512,1536]{1,0:T(8,128)} fusion(f32[512]{0:T(512)S(1)} %get-tuple-element.67), kind=kLoop, calls=%fused_computation.102 | loop fusion | flops 7864320 | bytes 3147776 | tf_op jit(solution)/shard_map/mul | solution.py:92
  51.8 14.1 %fusion.62 = (f32[512,1536]{1,0:T(8,128)}, f32[512,1536]{1,0:T(8,128)}) fusion(f32[512]{0:T(512)S(1)} %negate_multiply_fusion), kind=kLoop, calls=%fused_computation.88 | loop fusion | flops 8650752 | bytes 6293504 | tf_op jit(solution)/shard_map/mul | solution.py:94
  67.7 3.6 reshape.200
  71.3 13.4 %fusion.53 = f32[3,162,1536]{2,1,0:T(8,128)S(1)} fusion(f32[3,162,1024]{2,1,0:T(8,128)} %reshape.200, f32[512,1536]{1,0:T(8,128)S(1)} %copy-done.12, f32[512,1536]{1,0:T(8,128)} %fusion.71), kind=kOutput, calls=%fused_computation.78 | convolution fusion | flops 9174515712 | bytes 11268096 | tf_op jit(solution)/shard_map/pnl,lq->pnq/dot_general | solution.py:170
  84.7 4.0 %copy.83 = f32[3,162,1536]{2,0,1:T(4,128)} copy(f32[3,162,1536]{2,1,0:T(8,128)S(1)} %fusion.53) | data formatting | bytes 5971968 | tf_op jit(solution)/shard_map/pnl,lq->pnq/dot_general | solution.py:170
  92.2 2.5 mul.649
  96.9 2.5 mul.655
  99.4 3.5 copy.88
  102.9 13.4 %fusion.52 = f32[3,162,1536]{2,1,0:T(8,128)S(1)} fusion(f32[3,162,1024]{2,1,0:T(8,128)} %reshape.200, f32[512,1536]{1,0:T(8,128)} %get-tuple-element.60, f32[512,1536]{1,0:T(8,128)S(1)} %copy-done.11), kind=kOutput, calls=%fused_computation.77 | convolution fusion | flops 9174515712 | bytes 11268096 | tf_op jit(solution)/shard_map/pnl,lq->pnq/dot_general | solution.py:171
  116.3 4.2 %copy.89 = f32[3,162,1536]{2,0,1:T(4,128)} copy(f32[3,162,1536]{2,1,0:T(8,128)S(1)} %fusion.52) | data formatting | bytes 5971968 | tf_op jit(solution)/shard_map/pnl,lq->pnq/dot_general | solution.py:171
  120.5 9.5 %psum.35 = f32[]{:T(128)} all-reduce(f32[]{:T(128)} %get-tuple-element.35), channel_id=1, replica_groups=mesh['elem'=8,'mode'=4] {'mode'}, use_global_device_ids=true, to_apply=%region_1.2 | all-reduce | flops 1 | bytes 8 | tf_op jit(solution)/shard_map/psum | solution.py:187
  132.3 11.5 %fusion.16 = f32[3,2,9,1536,9]{3,4,2,1,0:T(8,128)} fusion(f32[9,9,1,1,1]{1,0,4,3,2:T(8,128)S(1)} %copy-done.14, f32[3,2,9,9,1536]{4,0,3,2,1:T(4,128)} %bitcast.133), kind=kOutput, calls=%fused_computation.24 | convolution fusion | flops 80621568 | bytes 5972292 | tf_op jit(solution)/shard_map/ij,peajq->peaiq/dot_general | solution.py:175
  143.8 14.0 %fusion.15 = f32[3,2,9,9,1536]{4,2,3,1,0:T(8,128)S(1)} fusion(f32[3,2,9,9,1536]{4,0,3,2,1:T(4,128)S(1)} %bitcast.135, f32[3,2,9,1536,9]{3,4,2,1,0:T(8,128)} %fusion.16, f32[9,9,1,1,1]{1,0,4,3,2:T(8,128)S(1)} %copy-done.14, f32[3,2,9,9,1536]{4,0,3,2,1:T(4,128)S(1)} %bitcast.134, f32[2,9,9,1536]{3,1,2,0:T(8,128)S(1)} %copy-done.3, f32[2]{0:T(128)S(1)} %copy-done.31, ...), kind=kOutput, calls=%fused_computation.20 | convolution fusion | flops 85847040 | bytes 14930256 | tf_op jit(solution)/shard_map/ij,pejbq->peibq/dot_general | solution.py:174
  160.8 17.4 %fusion.7 = f32[3,2,9,9,1024]{4,2,3,1,0:T(8,128)S(1)} fusion(f32[512,1536]{1,0:T(8,128)S(1)} %copy-done.10, f32[512,1536]{1,0:T(8,128)S(1)} %copy-done.9, f32[2,2,9,9,1536]{4,2,3,1,0:T(8,128)S(1)} %slice_negate_fusion, f32[1,2,9,9,1536]{4,2,3,1,0:T(8,128)S(1)} %slice_subtract_fusion), kind=kOutput, calls=%fused_computation.10 | convolution fusion | flops 9176835072 | bytes 11268096 | tf_op jit(solution)/shard_map/peabq,ql->peabl/dot_general | solution.py:198
  179.6 3.3 reshape.203
  182.8 3.0 constant_dynamic-slice_fusion
  185.8 3.3 collective-permute-start
  192.5 13.5 %collective-permute-done = f32[3,162,2,128]{3,2,0,1:T(2,128)} collective-permute-done((f32[3,162,2,128]{3,2,0,1:T(2,128)}, f32[3,162,2,128]{3,2,0,1:T(2,128)}, u32[]{:S(2)}, u32[]{:S(2)}) %collective-permute-start) | collective-permute-done | bytes 497696 | tf_op jit(solution)/shard_map/ppermute | solution.py:49
  207.3 16.1 %collective-permute-done.1 = f32[3,162,2,128]{3,2,0,1:T(2,128)S(1)} collective-permute-done((f32[3,162,2,128]{3,2,0,1:T(2,128)S(1)}, f32[3,162,2,128]{3,2,0,1:T(2,128)S(1)}, u32[]{:S(2)}, u32[]{:S(2)}) %collective-permute-start.1) | collective-permute-done | bytes 497696 | tf_op jit(solution)/shard_map/ppermute | solution.py:49
  223.6 8.7 %collective-permute-done.2 = f32[3,162,2,128]{3,2,0,1:T(2,128)S(1)} collective-permute-done((f32[3,162,2,128]{3,2,0,1:T(2,128)S(1)}, f32[3,162,2,128]{3,2,0,1:T(2,128)S(1)}, u32[]{:S(2)}, u32[]{:S(2)}) %collective-permute-start.2) | collective-permute-done | bytes 497696 | tf_op jit(solution)/shard_map/ppermute | solution.py:49
  232.5 2.6 multiply_add_fusion.1
  235.2 3.2 reshape.212
  240.7 2.6 collective-permute-start.4
  243.6 4.9 %collective-permute-done.3 = f32[3,8,1,9,256]{4,2,0,1,3:T(1,128)S(1)} collective-permute-done((f32[3,8,1,9,256]{4,2,0,1,3:T(1,128)S(1)}, f32[3,8,1,9,256]{4,2,0,1,3:T(1,128)S(1)}, u32[]{:S(2)}, u32[]{:S(2)}) %collective-permute-start.3) | collective-permute-done | bytes 221216 | tf_op jit(solution)/shard_map/ppermute | solution.py:61
  251.1 4.9 %fusion.45 = f32[3,8,9,256,9]{3,4,2,1,0:T(8,128)S(1)} fusion(f32[9,9,1,1,1]{1,0,4,3,2:T(8,128)S(1)} %copy-done.14, f32[3,8,9,9,256]{4,2,3,1,0:T(8,128)S(1)} %copy_multiply_fusion.5), kind=kOutput, calls=%fused_computation.65 | convolution fusion | flops 53747712 | bytes 3981636 | tf_op jit(solution)/shard_map/ij,peajl->peail/dot_general | solution.py:122
  256.0 4.2 %fusion.33 = f32[3,8,9,256,9]{3,4,2,1,0:T(8,128)S(1)} fusion(f32[9,9,1,1,1]{1,0,4,3,2:T(8,128)S(1)} %copy-done.14, f32[3,8,9,256,9]{3,4,2,1,0:T(8,128)S(1)} %fusion.45, f32[8]{0:T(128)S(1)} %copy-done.32, f32[9,9]{1,0:T(8,128)S(1)} %copy-done.18), kind=kOutput, calls=%fused_computation.49 | convolution fusion | flops 54743040 | bytes 3981992 | tf_op jit(solution)/shard_map/ji,peajl->peail/dot_general | solution.py:125
  260.2 4.0 %fusion.35 = f32[3,8,9,9,256]{4,2,3,1,0:T(8,128)S(1)} fusion(f32[9,9,1,1,1]{1,0,4,3,2:T(8,128)S(1)} %copy-done.14, f32[8]{0:T(128)S(1)} %copy-done.34, f32[9,9]{0,1:T(8,128)S(1)} %broadcast_multiply_fusion.5, f32[3,8,9,9,256]{4,2,0,1,3:T(8,128)S(1)} %fusion.25), kind=kOutput, calls=%fused_computation.52 | convolution fusion | flops 55240704 | bytes 3981992 | tf_op jit(solution)/shard_map/ij,pejbl->peibl/dot_general | solution.py:121
  264.2 6.0 %fusion.32 = f32[3,8,9,9,256]{4,2,0,1,3:T(8,128)S(1)} fusion(f32[3,8,9,256,9]{3,4,2,1,0:T(8,128)S(1)} %fusion.33, f32[8,9,9]{1,0,2:T(8,128)S(1)} %copy-done.23, f32[256]{0:T(256)S(1)} %pad_maximum_fusion.6, f32[3,8,9,1,256]{4,2,0,1,3:T(8,128)S(1)} %maximum_add_fusion.1, f32[3,8,1,9,256]{4,2,0,1,3:T(1,128)S(1)} %get-tuple-element.32, ...), kind=kOutput, calls=%fused_computation.48 | convolution fusion | flops 61212672 | bytes 8408932 | tf_op jit(solution)/shard_map/ji,pejbl->peibl/dot_general | solution.py:125
  270.5 2.6 collective-permute-start.6
  273.5 5.7 %collective-permute-done.5 = f32[3,8,1,9,256]{4,2,0,1,3:T(1,128)S(1)} collective-permute-done((f32[3,8,1,9,256]{4,2,0,1,3:T(1,128)S(1)}, f32[3,8,1,9,256]{4,2,0,1,3:T(1,128)S(1)}, u32[]{:S(2)}, u32[]{:S(2)}) %collective-permute-start.5) | collective-permute-done | bytes 221216 | tf_op jit(solution)/shard_map/ppermute | solution.py:61
  283.6 12.9 %all-reduce.1 = (f32[3,256]{1,0:T(4,128)}, f32[3,256]{1,0:T(4,128)}) all-reduce(f32[3,256]{1,0:T(4,128)} %get-tuple-element.8, f32[3,256]{1,0:T(4,128)} %get-tuple-element.7), channel_id=1, replica_groups=mesh['elem'=8,'mode'=4] {'elem'}, use_global_device_ids=true, to_apply=%region_4.5 | all-reduce | flops 1536 | bytes 12288 | tf_op jit(solution)/shard_map/psum | solution.py:139
  297.8 5.0 %multiply_subtract_fusion = (f32[3,8,9,9,256]{4,2,3,1,0:T(8,128)S(1)}, f32[3,8,9,9,256]{4,2,3,1,0:T(8,128)}) fusion(f32[3,256]{1,0:T(4,128)S(1)} %get-tuple-element.14, f32[3,8,9,9,256]{4,2,0,1,3:T(8,128)S(1)} %fusion.25, f32[3,8,9,1,256]{4,2,3,1,0:T(8,128)} %copy-done.8, f32[3,7,9,256]{3,2,0,1:T(8,128)} %copy-done.13, f32[3,1,9,256]{3,2,0,1:T(8,128)} %copy-done.15, ...), kind=kLoop, calls=%fused_computation.71 | loop fusion | flops 2543616 | bytes 7965696 | tf_op jit(solution)/shard_map/sub | solution.py:224
  302.8 4.9 %fusion.42 = f32[3,8,9,256,9]{3,4,2,1,0:T(8,128)S(1)} fusion(f32[9,9,1,1,1]{1,0,4,3,2:T(8,128)S(1)} %copy-done.14, f32[3,8,9,9,256]{4,2,3,1,0:T(8,128)S(1)} %get-tuple-element.25), kind=kOutput, calls=%fused_computation.61 | convolution fusion | flops 53747712 | bytes 3981636 | tf_op jit(solution)/shard_map/ij,peajl->peail/dot_general | solution.py:122
  307.8 3.4 fusion.30
  311.2 4.1 %fusion.28 = f32[3,8,9,256,9]{3,4,2,1,0:T(8,128)S(1)} fusion(f32[9,9,1,1,1]{1,0,4,3,2:T(8,128)S(1)} %copy-done.14, f32[3,8,9,256,9]{3,4,2,1,0:T(8,128)S(1)} %fusion.42, f32[8]{0:T(128)S(1)} %copy-done.33, f32[9,9]{1,0:T(8,128)S(1)} %copy-done.19), kind=kOutput, calls=%fused_computation.42 | convolution fusion | flops 54743040 | bytes 3981992 | tf_op jit(solution)/shard_map/ji,peajl->peail/dot_general | solution.py:125
  315.3 5.2 %fusion.27 = f32[3,8,9,9,256]{4,2,0,1,3:T(8,128)S(1)} fusion(f32[3,8,9,256,9]{3,4,2,1,0:T(8,128)S(1)} %fusion.28, f32[3,8,9,9,256]{4,2,3,1,0:T(8,128)S(1)} %get-tuple-element.25, f32[9,9,1,1,1]{1,0,2,3,4:T(8,128)S(1)} %copy-done.30, f32[3,8,9,9,256]{4,2,3,1,0:T(8,128)S(1)} %fusion.30, f32[256]{0:T(256)S(1)} %copy-done.41, f32[8,9,9]{1,0,2:T(8,128)S(1)} %copy-done.16), kind=kOutput, calls=%fused_computation.41 | convolution fusion | flops 56236032 | bytes 7966564 | tf_op jit(solution)/shard_map/ji,pejbl->peibl/dot_general | solution.py:125
  323.5 2.6 collective-permute-start.8
  326.1 3.0 copy.99
  329.1 4.7 %concatenate.89 = f32[3,648,2,128]{3,2,0,1:T(2,128)} reshape(f32[3,8,9,9,256]{4,0,3,2,1:T(4,128)} %copy.99) | data formatting | bytes 3981312 | tf_op jit(solution)/shard_map/concatenate | solution.py:110
  335.5 5.0 %copy.118 = f32[3,8,9,9,256]{4,0,3,2,1:T(4,128)} copy(f32[3,8,9,9,256]{4,2,3,1,0:T(8,128)} %get-tuple-element.26) | data formatting | bytes 3981312 | tf_op jit(solution)/shard_map/concatenate | solution.py:110
  340.5 4.5 %concatenate.105 = f32[3,648,2,128]{3,2,0,1:T(2,128)} reshape(f32[3,8,9,9,256]{4,0,3,2,1:T(4,128)} %copy.118) | data formatting | bytes 3981312 | tf_op jit(solution)/shard_map/concatenate | solution.py:110
  345.0 2.5 slice_add_fusion.1
  350.9 12.1 %all-reduce = (f32[3,256]{1,0:T(4,128)S(1)}, f32[3,256]{1,0:T(4,128)S(1)}) all-reduce(f32[3,256]{1,0:T(4,128)S(1)} %get-tuple-element.6, f32[3,256]{1,0:T(4,128)S(1)} %get-tuple-element.5), channel_id=1, replica_groups=mesh['elem'=8,'mode'=4] {'elem'}, use_global_device_ids=true, to_apply=%region_8.9 | all-reduce | flops 1536 | bytes 12288 | tf_op jit(solution)/shard_map/psum | solution.py:139
  363.2 3.6 multiply_add_fusion
  (169 shorter events, 41.9 us)
Async XLA Ops:
  0.0 9.5 %copy-start.38 = (f32[9]{0:T(128)S(1)}, f32[9]{0:T(128)}, u32[]{:S(2)}) copy-start(f32[9]{0:T(128)} %constant.83.clone) | copy-start | bytes 112
  0.0 9.7 %copy-start.39 = (f32[8]{0:T(128)S(1)}, f32[8]{0:T(128)}, u32[]{:S(2)}) copy-start(f32[8]{0:T(128)} %param.8) | copy-start | bytes 100
  0.0 9.7 %copy-start.36 = (s32[8]{0:T(128)S(1)}, s32[8]{0:T(128)}, u32[]{:S(2)}) copy-start(s32[8]{0:T(128)} %param.9) | copy-start | bytes 100
  3.6 62.4 %all-to-all-start = ((f32[3,648,2,128]{3,2,0,1:T(2,128)}), f32[3,648,2,128]{3,2,0,1:T(2,128)S(1)}, u32[]{:S(2)}, u32[]{:S(2)}) async-start(f32[3,648,2,128]{3,2,0,1:T(2,128)} %copy.80), calls=%async_computation | async-start | bytes 3981312 | tf_op jit(solution)/shard_map/all_to_all | solution.py:168
  9.7 29.4 %copy-start.17 = (f32[9,9]{1,0:T(8,128)}, f32[9,9]{1,0:T(8,128)S(1)}, u32[]{:S(2)}) copy-start(f32[9,9]{1,0:T(8,128)S(1)} %copy.79) | copy-start | bytes 976
  12.3 76.8 %copy-start.22 = (f32[1536]{0:T(1024)}, f32[1536]{0:T(1024)S(1)}, u32[]{:S(2)}) copy-start(f32[1536]{0:T(1024)S(1)} %fusion.75) | copy-start | bytes 18436
  67.7 3.6 copy-start.12
  99.4 3.5 copy-start.11
  116.3 16.0 %copy-start.14 = (f32[9,9,1,1,1]{1,0,4,3,2:T(8,128)S(1)}, f32[9,9,1,1,1]{1,0,4,3,2:T(8,128)}, u32[]{:S(2)}) copy-start(f32[9,9,1,1,1]{1,0,4,3,2:T(8,128)} %constant.85) | copy-start | bytes 976
  132.2 11.5 %copy-start.2 = (f32[3,162,1536]{2,0,1:T(4,128)S(1)}, f32[3,162,1536]{2,0,1:T(4,128)}, u32[]{:S(2)}) copy-start(f32[3,162,1536]{2,0,1:T(4,128)} %copy.83) | copy-start | bytes 8957956
  132.2 11.5 %copy-start.3 = (f32[2,9,9,1536]{3,1,2,0:T(8,128)S(1)}, f32[2,9,9,1536]{3,1,2,0:T(8,128)}, u32[]{:S(2)}) copy-start(f32[2,9,9,1536]{3,1,2,0:T(8,128)} %copy.88) | copy-start | bytes 2985988
  132.2 11.5 %copy-start.5 = (f32[3,162,1536]{2,0,1:T(4,128)S(1)}, f32[3,162,1536]{2,0,1:T(4,128)}, u32[]{:S(2)}) copy-start(f32[3,162,1536]{2,0,1:T(4,128)} %copy.89) | copy-start | bytes 8957956
  132.3 11.5 %copy-start.31 = (f32[2]{0:T(128)S(1)}, f32[2]{0:T(128)}, u32[]{:S(2)}) copy-start(f32[2]{0:T(128)} %get-tuple-element.66) | copy-start | bytes 28
  158.3 2.5 copy-start.9
  179.5 10.1 %copy-start.37 = (f32[8]{0:T(128)S(1)}, f32[8]{0:T(128)}, u32[]{:S(2)}) copy-start(f32[8]{0:T(128)} %get-tuple-element.63) | copy-start | bytes 100
  185.8 46.7 %copy-start.7 = (f32[3,648,2,128]{3,2,1,0:T(2,128)S(1)}, f32[3,648,2,128]{3,2,1,0:T(2,128)}, u32[]{:S(2)}) copy-start(f32[3,648,2,128]{3,2,1,0:T(2,128)} %param.6) | copy-start | bytes 5971972
  185.8 20.2 %collective-permute-start = (f32[3,162,2,128]{3,2,0,1:T(2,128)}, f32[3,162,2,128]{3,2,0,1:T(2,128)}, u32[]{:S(2)}, u32[]{:S(2)}) collective-permute-start(f32[3,162,2,128]{3,2,0,1:T(2,128)} %get-tuple-element.41), channel_id=1, source_target_pairs={{0,1},{1,0},{2,3},{3,2},{4,5},{5,4},{6,7},{7,6},{8,9},{9,8},{10,11... | collective-permute-start | bytes 1493000 | tf_op jit(solution)/shard_map/ppermute | solution.py:49
  190.3 33.1 %collective-permute-start.1 = (f32[3,162,2,128]{3,2,0,1:T(2,128)S(1)}, f32[3,162,2,128]{3,2,0,1:T(2,128)S(1)}, u32[]{:S(2)}, u32[]{:S(2)}) collective-permute-start(f32[3,162,2,128]{3,2,0,1:T(2,128)S(1)} %get-tuple-element.40), channel_id=1, source_target_pairs={{0,2},{1,3},{2,0},{3,1},{4,6},{5,7},{6,4},{7,5},{8,10},{9,11},{10,... | collective-permute-start | bytes 1493000 | tf_op jit(solution)/shard_map/ppermute | solution.py:49
  190.3 42.0 %collective-permute-start.2 = (f32[3,162,2,128]{3,2,0,1:T(2,128)S(1)}, f32[3,162,2,128]{3,2,0,1:T(2,128)S(1)}, u32[]{:S(2)}, u32[]{:S(2)}) collective-permute-start(f32[3,162,2,128]{3,2,0,1:T(2,128)S(1)} %get-tuple-element.39), channel_id=1, source_target_pairs={{0,3},{1,2},{2,1},{3,0},{4,7},{5,6},{6,5},{7,4},{8,11},{9,10},{10,... | collective-permute-start | bytes 1493000 | tf_op jit(solution)/shard_map/ppermute | solution.py:49
  238.4 5.0 %copy-start.42 = (f32[128]{0:T(128)S(1)}, f32[128]{0:T(128)}, u32[]{:S(2)}) copy-start(f32[128]{0:T(128)} %multiply_add_fusion.2) | copy-start | bytes 1540
  240.6 7.8 %collective-permute-start.3 = (f32[3,8,1,9,256]{4,2,0,1,3:T(1,128)S(1)}, f32[3,8,1,9,256]{4,2,0,1,3:T(1,128)S(1)}, u32[]{:S(2)}, u32[]{:S(2)}) collective-permute-start(f32[3,8,1,9,256]{4,2,0,1,3:T(1,128)S(1)} %get-tuple-element.33), channel_id=1, source_target_pairs={{0,4},{4,8},{8,12},{12,16},{16,20},{20,24},{24,28},{28,0},{1,5},{5... | collective-permute-start | bytes 663560 | tf_op jit(solution)/shard_map/ppermute | solution.py:61
  240.7 7.8 %collective-permute-start.4 = (f32[3,8,1,9,256]{4,2,0,1,3:T(1,128)S(1)}, f32[3,8,1,9,256]{4,2,0,1,3:T(1,128)S(1)}, u32[]{:S(2)}, u32[]{:S(2)}) collective-permute-start(f32[3,8,1,9,256]{4,2,0,1,3:T(1,128)S(1)} %get-tuple-element.34), channel_id=1, source_target_pairs={{4,0},{8,4},{12,8},{16,12},{20,16},{24,20},{28,24},{0,28},{5,1},{9... | collective-permute-start | bytes 663560 | tf_op jit(solution)/shard_map/ppermute | solution.py:62
  243.3 20.8 %copy-start.40 = (f32[256]{0:T(256)}, f32[256]{0:T(256)S(1)}, u32[]{:S(2)}) copy-start(f32[256]{0:T(256)S(1)} %pad_maximum_fusion.6) | copy-start | bytes 3076
  251.1 4.9 %copy-start.18 = (f32[9,9]{1,0:T(8,128)S(1)}, f32[9,9]{1,0:T(8,128)}, u32[]{:S(2)}) copy-start(f32[9,9]{1,0:T(8,128)} %copy-done.17) | copy-start | bytes 976
  251.1 4.9 %copy-start.32 = (f32[8]{0:T(128)S(1)}, f32[8]{0:T(128)}, u32[]{:S(2)}) copy-start(f32[8]{0:T(128)} %get-tuple-element.61) | copy-start | bytes 100
  256.0 4.2 %copy-start.34 = (f32[8]{0:T(128)S(1)}, f32[8]{0:T(128)}, u32[]{:S(2)}) copy-start(f32[8]{0:T(128)} %get-tuple-element.64) | copy-start | bytes 100
  260.2 4.0 %copy-start.23 = (f32[8,9,9]{1,0,2:T(8,128)S(1)}, f32[8,9,9]{1,0,2:T(8,128)}, u32[]{:S(2)}) copy-start(f32[8,9,9]{1,0,2:T(8,128)} %get-tuple-element.55) | copy-start | bytes 7780
  260.2 4.0 %copy-start.29 = (f32[9,9,1,1,1]{1,0,2,3,4:T(8,128)S(1)}, f32[9,9,1,1,1]{1,0,2,3,4:T(8,128)}, u32[]{:S(2)}) copy-start(f32[9,9,1,1,1]{1,0,2,3,4:T(8,128)} %constant.86) | copy-start | bytes 976
  270.4 8.7 %collective-permute-start.5 = (f32[3,8,1,9,256]{4,2,0,1,3:T(1,128)S(1)}, f32[3,8,1,9,256]{4,2,0,1,3:T(1,128)S(1)}, u32[]{:S(2)}, u32[]{:S(2)}) collective-permute-start(f32[3,8,1,9,256]{4,2,0,1,3:T(1,128)S(1)} %get-tuple-element.29), channel_id=1, source_target_pairs={{0,4},{4,8},{8,12},{12,16},{16,20},{20,24},{24,28},{28,0},{1,5},{5... | collective-permute-start | bytes 663560 | tf_op jit(solution)/shard_map/ppermute | solution.py:61
  270.5 8.6 %collective-permute-start.6 = (f32[3,8,1,9,256]{4,2,0,1,3:T(1,128)S(1)}, f32[3,8,1,9,256]{4,2,0,1,3:T(1,128)S(1)}, u32[]{:S(2)}, u32[]{:S(2)}) collective-permute-start(f32[3,8,1,9,256]{4,2,0,1,3:T(1,128)S(1)} %get-tuple-element.30), channel_id=1, source_target_pairs={{4,0},{8,4},{12,8},{16,12},{20,16},{24,20},{28,24},{0,28},{5,1},{9... | collective-permute-start | bytes 663560 | tf_op jit(solution)/shard_map/ppermute | solution.py:62
  273.2 7.5 %copy-start.20 = (f32[9,9]{0,1:T(8,128)}, f32[9,9]{0,1:T(8,128)S(1)}, u32[]{:S(2)}) copy-start(f32[9,9]{0,1:T(8,128)S(1)} %multiply_divide_fusion) | copy-start | bytes 976
  280.6 3.1 copy-start.13
  280.6 3.0 copy-start.15
  297.8 5.0 %copy-start.24 = (f32[3,256]{1,0:T(4,128)}, f32[3,256]{1,0:T(4,128)S(1)}, u32[]{:S(2)}) copy-start(f32[3,256]{1,0:T(4,128)S(1)} %get-tuple-element.14) | copy-start | bytes 9220
  302.8 12.4 %copy-start = (f32[3,8,9,9,256]{4,2,3,1,0:T(8,128)}, f32[3,8,9,9,256]{4,2,3,1,0:T(8,128)S(1)}, u32[]{:S(2)}) copy-start(f32[3,8,9,9,256]{4,2,3,1,0:T(8,128)S(1)} %get-tuple-element.25) | copy-start | bytes 5971972
  302.8 4.9 %copy-start.35 = (f32[8]{0:T(128)S(1)}, f32[8]{0:T(128)}, u32[]{:S(2)}) copy-start(f32[8]{0:T(128)} %get-tuple-element.64) | copy-start | bytes 100
  307.7 3.4 copy-start.19
  307.7 3.4 copy-start.33
  311.1 4.1 %copy-start.16 = (f32[8,9,9]{1,0,2:T(8,128)S(1)}, f32[8,9,9]{1,0,2:T(8,128)}, u32[]{:S(2)}) copy-start(f32[8,9,9]{1,0,2:T(8,128)} %get-tuple-element.56) | copy-start | bytes 7780
  311.2 4.1 %copy-start.30 = (f32[9,9,1,1,1]{1,0,2,3,4:T(8,128)S(1)}, f32[9,9,1,1,1]{1,0,2,3,4:T(8,128)}, u32[]{:S(2)}) copy-start(f32[9,9,1,1,1]{1,0,2,3,4:T(8,128)} %constant.86) | copy-start | bytes 976
  311.2 4.1 %copy-start.41 = (f32[256]{0:T(256)S(1)}, f32[256]{0:T(256)}, u32[]{:S(2)}) copy-start(f32[256]{0:T(256)} %copy-done.40) | copy-start | bytes 3076
  323.5 21.5 %collective-permute-start.7 = (f32[3,8,1,9,256]{4,2,0,1,3:T(1,128)}, f32[3,8,1,9,256]{4,2,0,1,3:T(1,128)}, u32[]{:S(2)}, u32[]{:S(2)}) collective-permute-start(f32[3,8,1,9,256]{4,2,0,1,3:T(1,128)} %get-tuple-element.23), channel_id=1, source_target_pairs={{0,4},{4,8},{8,12},{12,16},{16,20},{20,24},{24,28},{28,0},{1,5},{5... | collective-permute-start | bytes 663560 | tf_op jit(solution)/shard_map/ppermute | solution.py:61
  323.5 21.6 %collective-permute-start.8 = (f32[3,8,1,9,256]{4,2,0,1,3:T(1,128)}, f32[3,8,1,9,256]{4,2,0,1,3:T(1,128)}, u32[]{:S(2)}, u32[]{:S(2)}) collective-permute-start(f32[3,8,1,9,256]{4,2,0,1,3:T(1,128)} %get-tuple-element.24), channel_id=1, source_target_pairs={{4,0},{8,4},{12,8},{16,12},{20,16},{24,20},{28,24},{0,28},{5,1},{9... | collective-permute-start | bytes 663560 | tf_op jit(solution)/shard_map/ppermute | solution.py:62
  329.1 6.4 %copy-start.25 = (f32[3,256]{1,0:T(4,128)S(1)}, f32[3,256]{1,0:T(4,128)}, u32[]{:S(2)}) copy-start(f32[3,256]{1,0:T(4,128)} %copy-done.24) | copy-start | bytes 9220
  340.5 4.5 %copy-start.26 = (f32[3,256]{1,0:T(4,128)S(1)}, f32[3,256]{1,0:T(4,128)}, u32[]{:S(2)}) copy-start(f32[3,256]{1,0:T(4,128)} %get-tuple-element.13) | copy-start | bytes 9220
  347.6 2.0 copy-start.1
  349.6 13.5 %copy-start.27 = (f32[3,256]{1,0:T(4,128)S(1)}, f32[3,256]{1,0:T(4,128)}, u32[]{:S(2)}) copy-start(f32[3,256]{1,0:T(4,128)} %get-tuple-element.11) | copy-start | bytes 9220
  349.6 13.5 %copy-start.28 = (f32[3,256]{1,0:T(4,128)S(1)}, f32[3,256]{1,0:T(4,128)}, u32[]{:S(2)}) copy-start(f32[3,256]{1,0:T(4,128)} %get-tuple-element.12) | copy-start | bytes 9220
  (5 other events, 9.2 us)
